TPU v7x, 32 devices: a whole 2x2x4 slice. The times are simulated.
32 devices in a mesh: dp: 8 (over y, x, core), head: 4 (over z).
Axes of the slice: x: 2, y: 2, z: 4, core: 2. Of those that a mesh axis runs over, the one named last changes fastest.
Arguments:
- tokens_in: bfloat16 [16384, 768], P(('dp', 'head')), may hold values from -6 to 6
- gain_attn: float32 [768], replicated, may hold values from 0.1 to 1.9
- gain_ffn: float32 [768], replicated, may hold values from 0.1 to 1.9
- w_qkv: bfloat16 [3, 768, 768], P(None, None, 'head'), may hold values from -0.3125 to 0.3125
- w_out: bfloat16 [768, 768], P('head'), may hold values from -0.5 to 0.5
- w_up: bfloat16 [768, 768], replicated, may hold values from -0.21875 to 0.21875
- w_down: bfloat16 [768, 768], replicated, may hold values from -0.21875 to 0.21875
- slot_mol: int32 [8, 16], P('dp'), may hold values from 0 to 11, never falling along the last dimension, each value on 1 to 2 neighbouring positions
- slot_fill: int32 [8, 16], P('dp'), may hold values from 16 to 128
- cotangent: bfloat16 [16384, 768], P(('dp', 'head')), may hold values from -6 to 6
Outputs:
- layer_out: bfloat16 [16384, 768], P(('dp', 'head'))
- d_tokens: float32 [16384, 768], P(('dp', 'head'))
- d_gain_attn: float32 [768], replicated
- d_gain_ffn: float32 [768], replicated
- d_w_qkv: float32 [3, 768, 768], P(None, None, 'head')
- d_w_out: float32 [768, 768], P('head')
- d_w_up: float32 [768, 768], replicated
- d_w_down: float32 [768, 768], replicated
Inputs may be any that keep to these rules, and one draw needn't show every extreme that they name: `slot_mol`: each group holds 12 molecules numbered in slot order; a molecule takes one slot or two consecutive slots. `slot_fill`: the live tokens of a slot are its first rows.
All inputs are finite; a program needn't handle non-finite values.
Results may differ from a plain program's by a relative error of at most 0.015.
The roundings to bfloat16 on the way count: a program that leaves them out, or rounds other values in their place, can miss the bound.
Values may be sent and summed in bfloat16 or wider, within the bound.
A program may use at most 128 MiB of HBM per device.

v0:
```python
import jax
import jax.numpy as jnp
from jax import lax
from jax.sharding import PartitionSpec as P

HEAD_DIM = 24
SLOT_LEN = 128
epsilon = 1e-05
masked_score = -1000000000.0


def layer_norm(values, scale_gain):
    row_mean = jnp.mean(values, axis=-1, keepdims=True)
    centred = values - row_mean
    variance = jnp.mean(centred * centred, axis=-1, keepdims=True)
    return centred * lax.rsqrt(variance + epsilon) * scale_gain


def gelu_exact(values):
    return jax.nn.gelu(values, approximate=False)


def local(
    tokens_in, gain_attn, gain_ffn, w_qkv, w_out, w_up, w_down, slot_mol, slot_fill, cotangent
):
    rows_dev = tokens_in.shape[0]
    head_count = lax.axis_size("head")
    group_rows = rows_dev * head_count
    local_width = w_out.shape[0]
    local_heads = local_width // HEAD_DIM
    query_scale = HEAD_DIM ** (-0.5)
    block_rows = min(512, group_rows)
    block_count = group_rows // block_rows
    key_window = block_rows + 2 * SLOT_LEN
    padded_rows = group_rows + 2 * SLOT_LEN
    mol_rows = jnp.repeat(slot_mol[0], SLOT_LEN)
    fill_rows = jnp.repeat(slot_fill[0], SLOT_LEN)
    live_rows = jnp.arange(group_rows, dtype=jnp.int32) % SLOT_LEN < fill_rows
    mol_keys = jnp.pad(mol_rows, SLOT_LEN, constant_values=-1)
    live_keys = jnp.pad(live_rows, SLOT_LEN, constant_values=False)
    input_float = tokens_in.astype(jnp.float32)
    normed, norm_back = jax.vjp(layer_norm, input_float, gain_attn)
    normed_low = normed.astype(jnp.bfloat16)
    gathered = lax.all_gather(normed_low, "head", axis=0, tiled=True)
    column_scale = jnp.array([query_scale, 1.0, 1.0], jnp.float32)[:, None, None]
    projected = jnp.einsum("td,cde->cte", gathered, w_qkv, preferred_element_type=jnp.float32)
    projected_low = (projected * column_scale).astype(jnp.bfloat16)
    queries = projected_low[0].reshape(group_rows, local_heads, HEAD_DIM)
    pad_rows = ((SLOT_LEN, SLOT_LEN), (0, 0))
    keys_pad = jnp.pad(projected_low[1], pad_rows).reshape(padded_rows, local_heads, HEAD_DIM)
    values_pad = jnp.pad(projected_low[2], pad_rows).reshape(padded_rows, local_heads, HEAD_DIM)

    def scores_of(first_row):
        query_block = lax.dynamic_slice_in_dim(queries, first_row, block_rows, 0)
        key_block = lax.dynamic_slice_in_dim(keys_pad, first_row, key_window, 0)
        mol_block = lax.dynamic_slice_in_dim(mol_rows, first_row, block_rows, 0)
        mol_window = lax.dynamic_slice_in_dim(mol_keys, first_row, key_window, 0)
        live_window = lax.dynamic_slice_in_dim(live_keys, first_row, key_window, 0)
        allowed = (mol_block[:, None] == mol_window[None, :]) & live_window[None, :]
        raw_scores = jnp.einsum(
            "qhe,khe->hqk", query_block, key_block, preferred_element_type=jnp.float32
        )
        return jnp.where(allowed[None], raw_scores, masked_score)

    def attend(block_index):
        first_row = block_index * block_rows
        scores = scores_of(first_row)
        row_max = jnp.max(scores, axis=-1, keepdims=True)
        exp_scores = jnp.exp(scores - row_max)
        row_sum = jnp.sum(exp_scores, axis=-1, keepdims=True)
        probs_low = (exp_scores / row_sum).astype(jnp.bfloat16)
        value_block = lax.dynamic_slice_in_dim(values_pad, first_row, key_window, 0)
        mixed_block = jnp.einsum(
            "hqk,khe->qhe", probs_low, value_block, preferred_element_type=jnp.float32
        )
        return (
            mixed_block.reshape(block_rows, local_width).astype(jnp.bfloat16),
            (row_max + jnp.log(row_sum))[..., 0],
        )

    mixed_heads, log_sums = lax.map(attend, jnp.arange(block_count, dtype=jnp.int32))
    mixed_heads = mixed_heads.reshape(group_rows, local_width)
    mixed_rows = mixed_heads
    branch = lax.psum_scatter(
        jnp.dot(mixed_rows, w_out, preferred_element_type=jnp.float32),
        "head",
        scatter_dimension=0,
        tiled=True,
    )
    residual = input_float + branch
    normed_ffn, norm_ffn_back = jax.vjp(layer_norm, residual, gain_ffn)
    normed_ffn_low = normed_ffn.astype(jnp.bfloat16)
    ffn_inner = jnp.dot(normed_ffn_low, w_up, preferred_element_type=jnp.float32)
    activated, gelu_back = jax.vjp(gelu_exact, ffn_inner)
    hidden = activated.astype(jnp.bfloat16)
    output = (residual + jnp.dot(hidden, w_down, preferred_element_type=jnp.float32)).astype(
        jnp.bfloat16
    )
    grad_down = jnp.einsum("rf,rd->fd", hidden, cotangent, preferred_element_type=jnp.float32)
    d_hidden = jnp.einsum("rd,fd->rf", cotangent, w_down, preferred_element_type=jnp.float32)
    d_inner = gelu_back(d_hidden)[0].astype(jnp.bfloat16)
    grad_up = jnp.einsum("rd,rf->df", normed_ffn_low, d_inner, preferred_element_type=jnp.float32)
    d_normed_ffn = jnp.einsum("rf,df->rd", d_inner, w_up, preferred_element_type=jnp.float32)
    d_residual_norm, grad_gain_ffn = norm_ffn_back(d_normed_ffn)
    d_residual = cotangent.astype(jnp.float32) + d_residual_norm
    d_branch = d_residual.astype(jnp.bfloat16)
    shard_rows = lax.all_gather(d_branch, "head", axis=0, tiled=True)
    mixed_rows = mixed_heads
    grad_acc = jnp.einsum("te,td->ed", mixed_rows, shard_rows, preferred_element_type=jnp.float32)
    d_rows = jnp.einsum("td,ed->te", shard_rows, w_out, preferred_element_type=jnp.float32)
    grad_out = grad_acc
    d_mixed_low = d_rows.astype(jnp.bfloat16).reshape(group_rows, local_heads, HEAD_DIM)

    def back_block(running, block_index):
        d_key_acc, d_value_acc = running
        first_row = block_index * block_rows
        scores = scores_of(first_row)
        attn_probs = jnp.exp(scores - log_sums[block_index][:, :, None])
        probs_low = attn_probs.astype(jnp.bfloat16)
        query_block = lax.dynamic_slice_in_dim(queries, first_row, block_rows, 0)
        key_block = lax.dynamic_slice_in_dim(keys_pad, first_row, key_window, 0)
        value_block = lax.dynamic_slice_in_dim(values_pad, first_row, key_window, 0)
        grad_block = lax.dynamic_slice_in_dim(d_mixed_low, first_row, block_rows, 0)
        d_probs = jnp.einsum(
            "qhe,khe->hqk", grad_block, value_block, preferred_element_type=jnp.float32
        )
        inner_sum = jnp.sum(attn_probs * d_probs, axis=-1, keepdims=True)
        d_scores = (attn_probs * (d_probs - inner_sum)).astype(jnp.bfloat16)
        d_query = query_scale * jnp.einsum(
            "hqk,khe->qhe", d_scores, key_block, preferred_element_type=jnp.float32
        )
        d_key_block = jnp.einsum(
            "hqk,qhe->khe", d_scores, query_block, preferred_element_type=jnp.float32
        )
        d_value_block = jnp.einsum(
            "hqk,qhe->khe", probs_low, grad_block, preferred_element_type=jnp.float32
        )
        key_part = lax.dynamic_slice_in_dim(d_key_acc, first_row, key_window, 0)
        d_key_acc = lax.dynamic_update_slice_in_dim(d_key_acc, key_part + d_key_block, first_row, 0)
        value_part = lax.dynamic_slice_in_dim(d_value_acc, first_row, key_window, 0)
        d_value_acc = lax.dynamic_update_slice_in_dim(
            d_value_acc, value_part + d_value_block, first_row, 0
        )
        return ((d_key_acc, d_value_acc), d_query.astype(jnp.bfloat16))

    zero_pad = jnp.zeros((padded_rows, local_heads, HEAD_DIM), jnp.float32)
    (d_key_acc, d_value_acc), d_query = lax.scan(
        back_block, (zero_pad, zero_pad), jnp.arange(block_count, dtype=jnp.int32)
    )
    d_query = d_query.reshape(group_rows, local_width)
    d_key = (
        d_key_acc[SLOT_LEN : SLOT_LEN + group_rows]
        .reshape(group_rows, local_width)
        .astype(jnp.bfloat16)
    )
    d_value = (
        d_value_acc[SLOT_LEN : SLOT_LEN + group_rows]
        .reshape(group_rows, local_width)
        .astype(jnp.bfloat16)
    )
    d_qkv = jnp.stack([d_query, d_key, d_value])
    grad_qkv = jnp.einsum("td,cte->cde", gathered, d_qkv, preferred_element_type=jnp.float32)
    d_normed = lax.psum_scatter(
        jnp.einsum("cte,cde->td", d_qkv, w_qkv, preferred_element_type=jnp.float32).astype(
            jnp.bfloat16
        ),
        "head",
        scatter_dimension=0,
        tiled=True,
    ).astype(jnp.float32)
    d_input_norm, grad_gain_attn = norm_back(d_normed)
    d_tokens = d_residual + d_input_norm
    grad_qkv, grad_out = lax.psum((grad_qkv, grad_out), "dp")
    grad_up, grad_down, grad_gain_attn, grad_gain_ffn = lax.psum(
        (grad_up, grad_down, grad_gain_attn, grad_gain_ffn), ("dp", "head")
    )
    return (output, d_tokens, grad_gain_attn, grad_gain_ffn, grad_qkv, grad_out, grad_up, grad_down)


def solution(mesh):
    return jax.shard_map(
        local,
        mesh=mesh,
        in_specs=(
            P(("dp", "head"), None),
            P(),
            P(),
            P(None, None, "head"),
            P("head", None),
            P(),
            P(),
            P("dp", None),
            P("dp", None),
            P(("dp", "head"), None),
        ),
        out_specs=(
            P(("dp", "head"), None),
            P(("dp", "head"), None),
            P(),
            P(),
            P(None, None, "head"),
            P("head", None),
            P(),
            P(),
        ),
        check_vma=False,
    )
```

profile of v0, /device:TPU:0, one launch (start us, length us, event | category | flops | bytes accessed | tf_op | source)
XLA Modules:
  0.0 744.3 jit_solution(16228574355169517621)
XLA Ops:
  13.0 66.1 %all-gather.3.cloned.1.call-done = bf16[2048,768]{1,0:T(8,128)(2,1)} async-done(((bf16[512,768]{1,0:T(8,128)(2,1)}), bf16[2048,768]{1,0:T(8,128)(2,1)}) %all-gather.3.cloned.1.call-update) | async-done | bytes 3145744 | tf_op jit(solution)/shard_map/all_gather | solution.py:44
  85.8 52.1 %while.26 = (s32[]{:T(128)}, bf16[4,512,192]{1,2,0:T(8,128)(2,1)}, f32[4,8,512]{2,1,0:T(8,128)S(1)}, s32[4]{0:T(128)S(1)}, bf16[2304,8,24]{0,2,1:T(8,128)(2,1)},...) while((s32[]{:T(128)}, bf16[4,512,192]{1,2,0:T(8,128)(2,1)}, ...), condition=%wide.region_5.6_spmd, body=%wide.region_2.5_spmd.sunk | while | flops 331182080 | bytes 40846856 | solution.py:81
  93.6 4.5 fusion.122
  106.6 4.5 fusion.122
  119.6 4.5 fusion.122
  132.7 4.5 fusion.122
  143.9 109.4 %reduce-scatter.3.cloned.1.call-done = f32[512,768]{1,0:T(8,128)} async-done(((f32[2048,768]{1,0:T(8,128)}), f32[512,768]{1,0:T(8,128)}) %reduce-scatter.3.cloned.1.call-update) | async-done | bytes 1572880 | tf_op jit(solution)/shard_map/reduce_scatter | solution.py:84
  257.9 5.1 add_convert_fusion
  267.7 64.0 %all-gather.5.cloned.1.call-done = bf16[2048,768]{1,0:T(8,128)(2,1)} async-done(((bf16[512,768]{1,0:T(8,128)(2,1)}), bf16[2048,768]{1,0:T(8,128)(2,1)}) %all-gather.5.cloned.1.call-update) | async-done | bytes 3145744 | tf_op jit(solution)/shard_map/all_gather | solution.py:107
  337.4 104.5 %while.27 = (s32[]{:T(128)}, f32[2304,8,24]{0,2,1:T(8,128)}, f32[2304,8,24]{0,2,1:T(8,128)}, bf16[4,512,8,24]{1,3,2,0:T(8,128)(2,1)}, s32[4]{0:T(128)S(1)}, /*in...) while((s32[]{:T(128)}, f32[2304,8,24]{0,2,1:T(8,128)}, ...), condition=%wide.region_13.14_spmd, body=%wide.region_11.13_spmd.sunk | while | flops 793997312 | bytes 113673928 | solution.py:147
  344.1 4.5 fusion.133
  348.5 5.3 multiply_reduce_fusion.5
  370.2 4.5 fusion.133
  374.7 5.3 multiply_reduce_fusion.5
  396.3 4.5 fusion.133
  400.8 5.3 multiply_reduce_fusion.5
  422.4 4.5 fusion.133
  426.9 5.3 multiply_reduce_fusion.5
  448.8 4.1 bitcast_convert_fusion
  465.7 5.1 fusion.62
  470.8 41.3 %reduce-scatter.5.cloned.1.call-done = bf16[512,768]{1,0:T(8,128)(2,1)} async-done(((bf16[2048,768]{1,0:T(8,128)(2,1)}), bf16[512,768]{1,0:T(8,128)(2,1)}) %reduce-scatter.5.cloned.1.call-update) | async-done | bytes 786448 | tf_op jit(solution)/shard_map/reduce_scatter | solution.py:163
  517.1 40.9 %all-reduce.4 = (f32[768]{0:T(1024)}, f32[768]{0:T(1024)}) all-reduce(f32[768]{0:T(1024)} %get-tuple-element.137, f32[768]{0:T(1024)} %get-tuple-element.135), channel_id=1, replica_groups=mesh['dp'=8,'head'=4] {'dp','head'}, use_global_device_ids=true, to_apply=%region_18.19 | all-reduce | flops 1536 | bytes 12288 | tf_op jit(solution)/shard_map/psum | solution.py:174
  562.1 102.0 %all-reduce.10.cloned.1.call-done = (f32[768,768]{1,0:T(8,128)}, f32[768,768]{1,0:T(8,128)}) async-done(((f32[768,768]{1,0:T(8,128)}, f32[768,768]{1,0:T(8,128)}), (f32[768,768]{1,0:T(8,128)}, f32[768,768]{1,0:T(8,128)})) %all-reduce.10.cloned.1.call-update) | async-done | bytes 4718608 | tf_op jit(solution)/shard_map/psum | solution.py:174
  664.1 65.6 %all-reduce.12.cloned.1.call-done = (f32[3,768,192]{1,2,0:T(8,128)}, f32[192,768]{1,0:T(8,128)}) async-done(((f32[3,768,192]{1,2,0:T(8,128)}, f32[192,768]{1,0:T(8,128)}), (f32[3,768,192]{1,2,0:T(8,128)}, f32[192,768]{1,0:T(8,128)})) %all-reduce.12.cloned.1.call-update) | async-done | bytes 2359312 | tf_op jit(solution)/shard_map/psum | solution.py:173
  (266 shorter events, 155.9 us)
Async XLA Ops:
  7.2 250.5 %copy-start = (bf16[768,768]{1,0:T(8,128)(2,1)S(1)}, bf16[768,768]{1,0:T(8,128)(2,1)}, u32[]{:S(2)}) copy-start(bf16[768,768]{1,0:T(8,128)(2,1)} %param.21) | copy-start | bytes 3538948
  7.2 71.8 %all-gather.3.cloned.1.call-start = ((), (), s32[]{:S(2)}) async-start(), calls=%async_computation.2 | async-start | bytes 3932160 | tf_op jit(solution)/shard_map/all_gather | solution.py:44
  8.7 70.3 %copy-start.49 = (bf16[3,768,192]{1,2,0:T(8,128)(2,1)S(1)}, bf16[3,768,192]{1,2,0:T(8,128)(2,1)}, u32[]{:S(2)}) copy-start(bf16[3,768,192]{1,2,0:T(8,128)(2,1)} %param.18) | copy-start | bytes 2654212
  12.7 240.6 %reduce-scatter.3.cloned.1.call-start = ((), (), s32[]{:S(2)}) async-start(), calls=%async_computation.3 | async-start | bytes 7864320 | tf_op jit(solution)/shard_map/reduce_scatter | solution.py:84
  143.7 188.0 %all-gather.5.cloned.1.call-start = ((), (), s32[]{:S(2)}) async-start(), calls=%async_computation.4 | async-start | bytes 3932160 | tf_op jit(solution)/shard_map/all_gather | solution.py:107
  254.9 9.7 %copy-start.5 = (f32[512,768]{1,0:T(8,128)}, f32[512,768]{1,0:T(8,128)S(1)}, u32[]{:S(2)}) copy-start(f32[512,768]{1,0:T(8,128)S(1)} %get-tuple-element.196) | copy-start | bytes 4718596
  255.0 9.6 %copy-start.37 = (f32[512]{0:T(512)}, f32[512]{0:T(512)S(1)}, u32[]{:S(2)}) copy-start(f32[512]{0:T(512)S(1)} %broadcast_multiply_fusion) | copy-start | bytes 6148
  256.8 7.8 %copy-start.39 = (f32[512]{0:T(512)}, f32[512]{0:T(512)S(1)}, u32[]{:S(2)}) copy-start(f32[512]{0:T(512)S(1)} %fusion.72) | copy-start | bytes 6148
  267.6 244.6 %reduce-scatter.5.cloned.1.call-start = ((), (), s32[]{:S(2)}) async-start(), calls=%async_computation.5 | async-start | bytes 3932160 | tf_op jit(solution)/shard_map/reduce_scatter | solution.py:163
  337.4 6.6 copy-start.3
  337.4 6.6 copy-start.14
  363.6 6.6 copy-start.3
  363.6 6.6 copy-start.14
  389.7 6.6 copy-start.3
  389.7 6.6 copy-start.14
  415.8 6.6 copy-start.3
  415.8 6.6 copy-start.14
  453.0 211.2 %all-reduce.10.cloned.1.call-start = ((), (), s32[]{:S(2)}) async-start(), calls=%async_computation.6 | async-start | bytes 9437184 | tf_op jit(solution)/shard_map/psum | solution.py:174
  461.0 268.8 %all-reduce.12.cloned.1.call-start = ((), (), s32[]{:S(2)}) async-start(), calls=%async_computation.7 | async-start | bytes 4718592 | tf_op jit(solution)/shard_map/psum | solution.py:173
  470.8 41.4 %copy-start.2 = (bf16[512,768]{1,0:T(8,128)(2,1)S(1)}, bf16[512,768]{1,0:T(8,128)(2,1)}, u32[]{:S(2)}) copy-start(bf16[512,768]{1,0:T(8,128)(2,1)} %param.15) | copy-start | bytes 2359300
  470.8 41.4 %copy-start.32 = (f32[512]{0:T(512)S(1)}, f32[512]{0:T(512)}, u32[]{:S(2)}) copy-start(f32[512]{0:T(512)} %copy-done.31) | copy-start | bytes 6148
  470.8 41.4 %copy-start.34 = (f32[768]{0:T(1024)S(1)}, f32[768]{0:T(1024)}, u32[]{:S(2)}) copy-start(f32[768]{0:T(1024)} %param.16) | copy-start | bytes 9220
  470.8 43.7 %copy-start.36 = (f32[512]{0:T(512)S(1)}, f32[512]{0:T(512)}, u32[]{:S(2)}) copy-start(f32[512]{0:T(512)} %copy-done.35) | copy-start | bytes 6148
  470.8 87.9 %copy-start.8 = (f32[512,768]{1,0:T(8,128)S(1)}, f32[512,768]{1,0:T(8,128)}, u32[]{:S(2)}) copy-start(f32[512,768]{1,0:T(8,128)} %copy-done.7) | copy-start | bytes 4718596
  (45 other events, 113.5 us)
Sparse Core Ops, SparseCore 0:
  12.8 66.1 all-gather.2
  143.8 109.4 reduce-scatter.2
  267.7 63.9 all-gather.4
  453.1 59.0 reduce-scatter.4
  518.4 145.6 all-reduce.9
  667.9 61.8 all-reduce.11
where the time goes:
time: 746 us; the launch traced here: 744 us
  waiting for transfers between devices  449 us (60%)
  matrix products  143 us (19%)
  other arithmetic  46.8 us (6%)
  blocking collectives  40.9 us (5%)
  local copies, waits for them, and re-layouts  37.4 us (5%)
  between operations  14.6 us (2%)
  loops' own time  13.1 us (2%)
    reduce_scatter x1, waiting for transfers between devices, local(): lax.psum_scatter(jnp.dot(mixed_rows, w_out, preferred_element_type=jnp.fl...  109 us
    psum x1, waiting for transfers between devices, local(): lax.psum((grad_up, grad_down, grad_gain_attn, grad_gain_ffn), ('dp', 'hea...  102 us
    all_gather x1, waiting for transfers between devices, local(): gathered = lax.all_gather(normed_low, 'head', axis=0, tiled=True)  66.1 us
    psum x1, waiting for transfers between devices, local(): grad_qkv, grad_out = lax.psum((grad_qkv, grad_out), 'dp')  65.6 us
    all_gather x1, waiting for transfers between devices, local(): shard_rows = lax.all_gather(d_branch, 'head', axis=0, tiled=True)  64 us
    reduce_scatter x1, waiting for transfers between devices, local(): lax.psum_scatter(jnp.einsum('cte,cde->td', d_qkv, w_qkv, preferred_elemen...  41.3 us
    psum x1, blocking collectives, local(): lax.psum((grad_up, grad_down, grad_gain_attn, grad_gain_ffn), ('dp', 'hea...  40.9 us
    dot_general x8, matrix products, scores_of(): jnp.einsum('qhe,khe->hqk', query_block, key_block, preferred_element_type...  23.2 us
  transfers between devices with their start and end apart: 6, of which 6 were waited for; matrix products, arithmetic and copies ran while one was open for 3% of the time, Pallas kernels for 0%

commit v1 on v0

--- a/solution.py
+++ b/solution.py
@@ -7,6 +7,29 @@
 SLOT_LEN = 128
 epsilon = 1e-05
 masked_score = -1000000000.0
+
+
+def plan_the_cycles(work_x, at_axis):
+    work_x = jnp.moveaxis(work_x, 0, at_axis)
+    outer = work_x.shape
+    return work_x.reshape(
+        *outer[:at_axis], outer[at_axis] * outer[at_axis + 1], *outer[at_axis + 2 :]
+    )
+
+
+def remake_pages(piece_in, axis_id):
+    y_new = lax.axis_size(axis_id)
+    back = lax.axis_index(axis_id)
+    y1, o_now = (y_new, back)
+    everything, p_next = (piece_in[None], 1)
+    while p_next < y1:
+        piece_now = lax.ppermute(everything, axis_id, [(dev, dev ^ p_next) for dev in range(y1)])
+        mid_arr = o_now & p_next == 0
+        earlier = jnp.where(mid_arr, everything, piece_now)
+        inter = jnp.where(mid_arr, piece_now, everything)
+        everything = jnp.concatenate([earlier, inter])
+        p_next *= 2
+    return everything
 
 
 def layer_norm(values, scale_gain):
@@ -41,7 +64,8 @@
     input_float = tokens_in.astype(jnp.float32)
     normed, norm_back = jax.vjp(layer_norm, input_float, gain_attn)
     normed_low = normed.astype(jnp.bfloat16)
-    gathered = lax.all_gather(normed_low, "head", axis=0, tiled=True)
+    val2 = remake_pages(normed_low, "head")
+    gathered = plan_the_cycles(val2, 0)
     column_scale = jnp.array([query_scale, 1.0, 1.0], jnp.float32)[:, None, None]
     projected = jnp.einsum("td,cde->cte", gathered, w_qkv, preferred_element_type=jnp.float32)
     projected_low = (projected * column_scale).astype(jnp.bfloat16)

time: 746 us -> 783 us (1.050)
  starting transfers between devices: 0.43 us -> 17.4 us
  waiting for transfers between devices: 449 us -> 458 us
    ppermute x0 -> x2, waiting for transfers between devices: none -> 84.6 us  [remake_pages(): lax.ppermute(everything, axis_id, [(dev, dev ^ p_next) for dev in range(y...]
    all_gather x1 -> x0, waiting for transfers between devices: 66.1 us -> none  [local(): gathered = lax.all_gather(normed_low, 'head', axis=0, tiled=True)]
    all_gather x1, starting transfers between devices: 0.22 us -> 11.4 us  [local(): shard_rows = lax.all_gather(d_branch, 'head', axis=0, tiled=True)]
    reduce_scatter x1, waiting for transfers between devices: 109 us -> 101 us  [local(): lax.psum_scatter(jnp.dot(mixed_rows, w_out, preferred_element_type=jnp.fl...]
    unnamed x98 -> x106, local copies, waits for them, and re-layouts: 15.4 us -> 16.8 us
  transfers between devices with their start and end apart: 6 -> 7, of which waited for: 6 -> 7; matrix products, arithmetic and copies ran while one was open for 3% -> 3% of each run, Pallas kernels for 0% -> 0%
where the time goes in v1:
time: 783 us; the launch traced here: 774 us
  waiting for transfers between devices  458 us (58%)
  matrix products  140 us (18%)
  other arithmetic  50.6 us (6%)
  blocking collectives  40.9 us (5%)
  local copies, waits for them, and re-layouts  39 us (5%)
  starting transfers between devices  17.4 us (2%)
  between operations  14.7 us (2%)
  loops' own time  12.9 us (2%)
    psum x1, waiting for transfers between devices, local(): lax.psum((grad_up, grad_down, grad_gain_attn, grad_gain_ffn), ('dp', 'hea...  102 us
    reduce_scatter x1, waiting for transfers between devices, local(): lax.psum_scatter(jnp.dot(mixed_rows, w_out, preferred_element_type=jnp.fl...  101 us
    ppermute x2, waiting for transfers between devices, remake_pages(): lax.ppermute(everything, axis_id, [(dev, dev ^ p_next) for dev in range(y...  84.6 us
    psum x1, waiting for transfers between devices, local(): grad_qkv, grad_out = lax.psum((grad_qkv, grad_out), 'dp')  65.6 us
    all_gather x1, waiting for transfers between devices, local(): shard_rows = lax.all_gather(d_branch, 'head', axis=0, tiled=True)  64.1 us
    reduce_scatter x1, waiting for transfers between devices, local(): lax.psum_scatter(jnp.einsum('cte,cde->td', d_qkv, w_qkv, preferred_elemen...  41.5 us
    psum x1, blocking collectives, local(): lax.psum((grad_up, grad_down, grad_gain_attn, grad_gain_ffn), ('dp', 'hea...  40.9 us
    dot_general x8, matrix products, scores_of(): jnp.einsum('qhe,khe->hqk', query_block, key_block, preferred_element_type...  23.2 us
  transfers between devices with their start and end apart: 7, of which 7 were waited for; matrix products, arithmetic and copies ran while one was open for 3% of the time, Pallas kernels for 0%

profile of v1, /device:TPU:0, one launch (start us, length us, event | category | flops | bytes accessed | tf_op | source)
XLA Modules:
  0.0 773.8 jit_solution(8368778512674738803)
XLA Ops:
  14.2 17.6 %collective-permute-done = bf16[1,512,768]{2,1,0:T(8,128)(2,1)} collective-permute-done((bf16[1,512,768]{2,1,0:T(8,128)(2,1)S(1)}, bf16[1,512,768]{2,1,0:T(8,128)(2,1)}, u32[]{:S(2)}, u32[]{:S(2)}) %collective-permute-start) | collective-permute-done | bytes 786464 | tf_op jit(solution)/shard_map/ppermute | solution.py:26
  38.4 67.0 %collective-permute-done.1 = bf16[2,512,768]{2,1,0:T(8,128)(2,1)} collective-permute-done((bf16[2,512,768]{2,1,0:T(8,128)(2,1)}, bf16[2,512,768]{2,1,0:T(8,128)(2,1)}, u32[]{:S(2)}, u32[]{:S(2)}) %collective-permute-start.1) | collective-permute-done | bytes 1572896 | tf_op jit(solution)/shard_map/ppermute | solution.py:26
  112.9 52.1 %while.26 = (s32[]{:T(128)}, bf16[4,512,192]{1,2,0:T(8,128)(2,1)}, f32[4,8,512]{2,1,0:T(8,128)S(1)}, s32[4]{0:T(128)S(1)}, bf16[2304,8,24]{0,2,1:T(8,128)(2,1)},...) while((s32[]{:T(128)}, bf16[4,512,192]{1,2,0:T(8,128)(2,1)}, ...), condition=%wide.region_5.6_spmd, body=%wide.region_2.5_spmd.sunk | while | flops 331182080 | bytes 40846856 | solution.py:105
  120.8 4.5 fusion.119
  133.8 4.5 fusion.119
  146.8 4.5 fusion.119
  159.8 4.5 fusion.119
  170.9 11.4 %all-gather.2.cloned.1.call-start = ((), (), s32[]{:S(2)}) async-start(), calls=%async_computation.3 | async-start | bytes 3932160 | tf_op jit(solution)/shard_map/all_gather | solution.py:131
  182.3 100.5 %reduce-scatter.3.cloned.1.call-done = f32[512,768]{1,0:T(8,128)} async-done(((f32[2048,768]{1,0:T(8,128)}), f32[512,768]{1,0:T(8,128)}) %reduce-scatter.3.cloned.1.call-update) | async-done | bytes 1572880 | tf_op jit(solution)/shard_map/reduce_scatter | solution.py:108
  287.4 5.1 add_convert_fusion
  297.2 64.1 %all-gather.2.cloned.1.call-done = bf16[2048,768]{1,0:T(8,128)(2,1)} async-done(((bf16[512,768]{1,0:T(8,128)(2,1)}), bf16[2048,768]{1,0:T(8,128)(2,1)}) %all-gather.2.cloned.1.call-update) | async-done | bytes 3145744 | tf_op jit(solution)/shard_map/all_gather | solution.py:131
  367.0 104.5 %while.27 = (s32[]{:T(128)}, f32[2304,8,24]{0,2,1:T(8,128)}, f32[2304,8,24]{0,2,1:T(8,128)}, bf16[4,512,8,24]{1,3,2,0:T(8,128)(2,1)}, s32[4]{0:T(128)S(1)}, /*in...) while((s32[]{:T(128)}, f32[2304,8,24]{0,2,1:T(8,128)}, ...), condition=%wide.region_13.14_spmd, body=%wide.region_11.13_spmd.sunk | while | flops 793997312 | bytes 113673928 | solution.py:171
  373.6 4.5 fusion.130
  378.1 5.3 multiply_reduce_fusion.5
  399.7 4.5 fusion.130
  404.2 5.3 multiply_reduce_fusion.5
  425.9 4.5 fusion.130
  430.3 5.3 multiply_reduce_fusion.5
  452.0 4.5 fusion.130
  456.5 5.3 multiply_reduce_fusion.5
  500.2 41.5 %reduce-scatter.5.cloned.1.call-done = bf16[512,768]{1,0:T(8,128)(2,1)} async-done(((bf16[2048,768]{1,0:T(8,128)(2,1)}), bf16[512,768]{1,0:T(8,128)(2,1)}) %reduce-scatter.5.cloned.1.call-update) | async-done | bytes 786448 | tf_op jit(solution)/shard_map/reduce_scatter | solution.py:187
  546.7 40.9 %all-reduce.4 = (f32[768]{0:T(1024)}, f32[768]{0:T(1024)}) all-reduce(f32[768]{0:T(1024)} %get-tuple-element.137, f32[768]{0:T(1024)} %get-tuple-element.135), channel_id=1, replica_groups=mesh['dp'=8,'head'=4] {'dp','head'}, use_global_device_ids=true, to_apply=%region_18.19 | all-reduce | flops 1536 | bytes 12288 | tf_op jit(solution)/shard_map/psum | solution.py:198
  591.6 102.0 %all-reduce.10.cloned.1.call-done = (f32[768,768]{1,0:T(8,128)}, f32[768,768]{1,0:T(8,128)}) async-done(((f32[768,768]{1,0:T(8,128)}, f32[768,768]{1,0:T(8,128)}), (f32[768,768]{1,0:T(8,128)}, f32[768,768]{1,0:T(8,128)})) %all-reduce.10.cloned.1.call-update) | async-done | bytes 4718608 | tf_op jit(solution)/shard_map/psum | solution.py:198
  693.7 65.6 %all-reduce.12.cloned.1.call-done = (f32[3,768,192]{1,2,0:T(8,128)}, f32[192,768]{1,0:T(8,128)}) async-done(((f32[3,768,192]{1,2,0:T(8,128)}, f32[192,768]{1,0:T(8,128)}), (f32[3,768,192]{1,2,0:T(8,128)}, f32[192,768]{1,0:T(8,128)})) %all-reduce.12.cloned.1.call-update) | async-done | bytes 2359312 | tf_op jit(solution)/shard_map/psum | solution.py:197
  (279 shorter events, 173.5 us)
Async XLA Ops:
  7.2 280.0 %copy-start = (bf16[768,768]{1,0:T(8,128)(2,1)S(1)}, bf16[768,768]{1,0:T(8,128)(2,1)}, u32[]{:S(2)}) copy-start(bf16[768,768]{1,0:T(8,128)(2,1)} %param.21) | copy-start | bytes 3538948
  7.2 275.6 %reduce-scatter.3.cloned.1.call-start = ((), (), s32[]{:S(2)}) async-start(), calls=%async_computation.2 | async-start | bytes 7864320 | tf_op jit(solution)/shard_map/reduce_scatter | solution.py:108
  8.7 24.8 %copy-start.37 = (f32[512]{0:T(512)}, f32[512]{0:T(512)S(1)}, u32[]{:S(2)}) copy-start(f32[512]{0:T(512)S(1)} %broadcast_multiply_fusion.1) | copy-start | bytes 6148
  10.8 22.7 %copy-start.39 = (f32[512]{0:T(512)}, f32[512]{0:T(512)S(1)}, u32[]{:S(2)}) copy-start(f32[512]{0:T(512)S(1)} %fusion.67) | copy-start | bytes 6148
  11.1 20.8 %collective-permute-start = (bf16[1,512,768]{2,1,0:T(8,128)(2,1)S(1)}, bf16[1,512,768]{2,1,0:T(8,128)(2,1)}, u32[]{:S(2)}, u32[]{:S(2)}) collective-permute-start(bf16[1,512,768]{2,1,0:T(8,128)(2,1)S(1)} %fusion.62), channel_id=1, source_target_pairs={{0,1},{1,0},{2,3},{3,2},{4,5},{5,4},{6,7},{7,6},{8,9},{9,8},{10,11... | collective-permute-start | bytes 2359304 | tf_op jit(solution)/shard_map/ppermute | solution.py:26
  34.9 70.5 %collective-permute-start.1 = (bf16[2,512,768]{2,1,0:T(8,128)(2,1)}, bf16[2,512,768]{2,1,0:T(8,128)(2,1)}, u32[]{:S(2)}, u32[]{:S(2)}) collective-permute-start(bf16[2,512,768]{2,1,0:T(8,128)(2,1)} %pad_maximum_fusion.2), channel_id=1, source_target_pairs={{0,2},{1,3},{2,0},{3,1},{4,6},{5,7},{6,4},{7,5},{8,10},{9,11},{10,... | collective-permute-start | bytes 4718600 | tf_op jit(solution)/shard_map/ppermute | solution.py:26
  170.9 190.4 %all-gather.2.cloned.1.call-start = ((), (), s32[]{:S(2)}) async-start(), calls=%async_computation.3 | async-start | bytes 3932160 | tf_op jit(solution)/shard_map/all_gather | solution.py:131
  284.4 9.7 %copy-start.5 = (f32[512,768]{1,0:T(8,128)}, f32[512,768]{1,0:T(8,128)S(1)}, u32[]{:S(2)}) copy-start(f32[512,768]{1,0:T(8,128)S(1)} %get-tuple-element.196) | copy-start | bytes 4718596
  284.5 9.6 %copy-start.41 = (f32[512]{0:T(512)}, f32[512]{0:T(512)S(1)}, u32[]{:S(2)}) copy-start(f32[512]{0:T(512)S(1)} %broadcast_multiply_fusion) | copy-start | bytes 6148
  286.3 7.8 %copy-start.43 = (f32[512]{0:T(512)}, f32[512]{0:T(512)S(1)}, u32[]{:S(2)}) copy-start(f32[512]{0:T(512)S(1)} %fusion.68) | copy-start | bytes 6148
  297.1 244.6 %reduce-scatter.5.cloned.1.call-start = ((), (), s32[]{:S(2)}) async-start(), calls=%async_computation.4 | async-start | bytes 3932160 | tf_op jit(solution)/shard_map/reduce_scatter | solution.py:187
  393.1 6.6 copy-start.3
  393.1 6.6 copy-start.14
  419.2 6.6 copy-start.3
  419.2 6.6 copy-start.14
  445.4 6.6 copy-start.3
  445.4 6.6 copy-start.14
  482.5 211.2 %all-reduce.10.cloned.1.call-start = ((), (), s32[]{:S(2)}) async-start(), calls=%async_computation.5 | async-start | bytes 9437184 | tf_op jit(solution)/shard_map/psum | solution.py:198
  490.5 268.8 %all-reduce.12.cloned.1.call-start = ((), (), s32[]{:S(2)}) async-start(), calls=%async_computation.6 | async-start | bytes 4718592 | tf_op jit(solution)/shard_map/psum | solution.py:197
  500.2 41.5 %copy-start.2 = (bf16[512,768]{1,0:T(8,128)(2,1)S(1)}, bf16[512,768]{1,0:T(8,128)(2,1)}, u32[]{:S(2)}) copy-start(bf16[512,768]{1,0:T(8,128)(2,1)} %param.15) | copy-start | bytes 2359300
  500.2 41.5 %copy-start.36 = (f32[768]{0:T(1024)S(1)}, f32[768]{0:T(1024)}, u32[]{:S(2)}) copy-start(f32[768]{0:T(1024)} %param.16) | copy-start | bytes 9220
  500.2 41.5 %copy-start.38 = (f32[512]{0:T(512)S(1)}, f32[512]{0:T(512)}, u32[]{:S(2)}) copy-start(f32[512]{0:T(512)} %copy-done.37) | copy-start | bytes 6148
  500.2 43.8 %copy-start.40 = (f32[512]{0:T(512)S(1)}, f32[512]{0:T(512)}, u32[]{:S(2)}) copy-start(f32[512]{0:T(512)} %copy-done.39) | copy-start | bytes 6148
  500.2 88.0 %copy-start.8 = (f32[512,768]{1,0:T(8,128)S(1)}, f32[512,768]{1,0:T(8,128)}, u32[]{:S(2)}) copy-start(f32[512,768]{1,0:T(8,128)} %copy-done.7) | copy-start | bytes 4718596
  (50 other events, 132.4 us)
Sparse Core Ops, SparseCore 0:
  171.0 111.7 reduce-scatter.2
  297.2 63.9 all-gather.1
  482.6 59.0 reduce-scatter.4
  547.9 145.6 all-reduce.9
  697.4 61.7 all-reduce.11
